TPU v7x, 128 devices: a whole 4x4x4 slice. The times are simulated.
128 devices in a mesh: row: 16 (over y, z), col: 8 (over x, core).
Axes of the slice: x: 4, y: 4, z: 4, core: 2. Of those that a mesh axis runs over, the one named last changes fastest.
Arguments:
- tokens: bfloat16 [2048, 4096], P('row', 'col'), may hold values from -6 to 6
- w_in: bfloat16 [4096, 16384], P('col', 'row'), may hold values from -0.09375 to 0.09375
- w_out: bfloat16 [16384, 4096], P('row', 'col'), may hold values from -0.046875 to 0.046875
- cotangent: bfloat16 [2048, 4096], P('row', 'col'), may hold values from -6 to 6
Outputs:
- block_out: bfloat16 [2048, 4096], P(('row', 'col'))
- grad_tokens: bfloat16 [2048, 4096], P('row', 'col')
- grad_in: float32 [4096, 16384], P('col', 'row')
- grad_out: float32 [16384, 4096], P('row', 'col')
All inputs are finite; a program needn't handle non-finite values.
Results may differ from a plain program's by a relative error of at most 0.015.
Values may be sent and summed in bfloat16 or wider, within the bound.
A program may use at most 128 MiB of HBM per device.

v0:
```python
import jax
import jax.numpy as jnp
from jax import lax
from jax.sharding import PartitionSpec as P


def gelu_grad(value):
    cdf = 0.5 * (1.0 + jax.scipy.special.erf(value * 0.7071067811865476))
    pdf = jnp.exp(-0.5 * value * value) * 0.3989422804014327
    return cdf + value * pdf


def token_panel(local_rows):
    return lax.all_gather(local_rows, "row", axis=0, tiled=True)


def token_panel_a2a(local_rows):
    n = lax.axis_size("row")
    copies = jnp.broadcast_to(local_rows[None], (n,) + local_rows.shape)
    copies = copies.reshape(n * local_rows.shape[0], local_rows.shape[1])
    return lax.all_to_all(copies, "row", split_axis=0, concat_axis=0, tiled=True)


def hidden_panel(local_rows):
    return lax.all_gather(local_rows, "col", axis=0, tiled=True)


def contract_last(left, right):
    return lax.dot_general(
        left, right, (((1,), (1,)), ((), ())), preferred_element_type=jnp.float32
    )


def width_split(left_all, right, transposed):
    if transposed:
        term = contract_last(left_all, right)
    else:
        term = jnp.dot(left_all, right, preferred_element_type=jnp.float32)
    return lax.psum_scatter(
        term.astype(jnp.bfloat16), "col", scatter_dimension=0, tiled=True
    ).astype(jnp.float32)


def unit_sum(left_all, right, transposed):
    n = lax.axis_size("row")
    if transposed:
        term = contract_last(left_all, right)
    else:
        term = jnp.dot(left_all, right, preferred_element_type=jnp.float32)
    pieces = term.astype(jnp.bfloat16).reshape(n, term.shape[0] // n, term.shape[1])
    pieces = lax.all_to_all(pieces, "row", split_axis=0, concat_axis=0, tiled=True)
    return jnp.sum(pieces.astype(jnp.float32), axis=0)


def local(tokens, w_in, w_out, cotangent):
    tokens_all = token_panel(tokens)
    upstream_all = token_panel_a2a(cotangent)
    pre_part = width_split(tokens_all, w_in, False)
    act_all = hidden_panel(jax.nn.gelu(pre_part, approximate=False).astype(jnp.bfloat16))
    dact_part = width_split(upstream_all, w_out, True)
    dpre_all = hidden_panel((dact_part * gelu_grad(pre_part)).astype(jnp.bfloat16))
    mixed = unit_sum(act_all, w_out, False)
    block_rows = (tokens.astype(jnp.float32) + mixed).astype(jnp.bfloat16)
    block_out = lax.all_to_all(block_rows, "col", split_axis=0, concat_axis=1, tiled=True)
    grad_out = lax.dot_general(
        act_all, upstream_all, (((0,), (0,)), ((), ())), preferred_element_type=jnp.float32
    )
    grad_in = lax.dot_general(
        tokens_all, dpre_all, (((0,), (0,)), ((), ())), preferred_element_type=jnp.float32
    )
    back = unit_sum(dpre_all, w_in, True)
    grad_tokens = (cotangent.astype(jnp.float32) + back).astype(jnp.bfloat16)
    return (block_out, grad_tokens, grad_in, grad_out)


def solution(mesh):
    in_specs = (P("row", "col"), P("col", "row"), P("row", "col"), P("row", "col"))
    out_specs = (P(("row", "col"), None), P("row", "col"), P("col", "row"), P("row", "col"))
    return jax.shard_map(local, mesh=mesh, in_specs=in_specs, out_specs=out_specs, check_vma=False)
```

profile of v0, /device:TPU:1, one launch (start us, length us, event | category | flops | bytes accessed | tf_op | source)
XLA Modules:
  0.0 260.2 jit_solution(16874489885100301524)
XLA Ops:
  8.0 0.0 copy-start
  8.0 0.0 all-gather.4.cloned.1.call-start
  8.1 0.7 all-gather.4.cloned.1.call-update
  8.7 0.0 reduce-scatter.5.cloned.1.call-start
  8.8 1.1 broadcast_in_dim.2
  9.9 37.6 %all_to_all.38 = bf16[16,128,512]{2,1,0:T(8,128)(2,1)S(1)} all-to-all(bf16[16,128,512]{2,1,0:T(8,128)(2,1)S(1)} %broadcast_in_dim.2), channel_id=1, replica_groups=mesh['row'=16,'col'=8] {'row'}, dimensions={0} | all-to-all | bytes 4194304 | tf_op jit(solution)/shard_map/all_to_all | solution.py:21
  47.5 0.0 copy-start.1
  47.5 1.4 copy-done.1
  48.9 0.0 copy-done
  48.9 4.3 %convolution_convert_fusion = bf16[2048,1024]{1,0:T(8,128)(2,1)} fusion(bf16[2048,512]{1,0:T(8,128)(2,1)S(1)} %bitcast.21, bf16[1024,512]{1,0:T(8,128)(2,1)S(1)} %copy-done), kind=kOutput, calls=%fused_computation.2 | convolution fusion | flops 2149580800 | bytes 7340032 | tf_op jit(solution)/shard_map/dot_general | solution.py:29
  53.2 0.0 copy-start.4
  53.2 0.0 reduce-scatter.5.cloned.1.call-update
  53.3 0.0 reduce-scatter.3.cloned.1.call-start
  53.3 12.5 %all-gather.4.cloned.1.call-done = bf16[2048,512]{1,0:T(8,128)(2,1)} async-done(((bf16[128,512]{1,0:T(8,128)(2,1)}), bf16[2048,512]{1,0:T(8,128)(2,1)}) %all-gather.4.cloned.1.call-update) | async-done | bytes 2097168 | tf_op jit(solution)/shard_map/all_gather | solution.py:14
  65.8 0.0 copy-done.4
  65.8 5.9 %convolution_convert_fusion.1 = bf16[2048,1024]{1,0:T(8,128)(2,1)} fusion(bf16[2048,512]{1,0:T(8,128)(2,1)} %all-gather.4.cloned.1.call-done, bf16[512,1024]{1,0:T(8,128)(2,1)S(1)} %copy-done.4), kind=kOutput, calls=%fused_computation.3 | convolution fusion | flops 2149580800 | bytes 7340032 | tf_op jit(solution)/shard_map/dot_general | solution.py:38
  71.8 0.0 reduce-scatter.3.cloned.1.call-update
  71.8 0.0 all-gather.6.cloned.1.call-start
  71.9 15.8 %reduce-scatter.5.cloned.1.call-done = bf16[256,1024]{1,0:T(8,128)(2,1)} async-done(((bf16[2048,1024]{1,0:T(8,128)(2,1)}), bf16[256,1024]{1,0:T(8,128)(2,1)}) %reduce-scatter.5.cloned.1.call-update) | async-done | bytes 524304 | tf_op jit(solution)/shard_map/reduce_scatter | solution.py:39
  87.7 38.8 %reduce-scatter.3.cloned.1.call-done = bf16[256,1024]{1,0:T(8,128)(2,1)} async-done(((bf16[2048,1024]{1,0:T(8,128)(2,1)}), bf16[256,1024]{1,0:T(8,128)(2,1)}) %reduce-scatter.3.cloned.1.call-update) | async-done | bytes 524304 | tf_op jit(solution)/shard_map/reduce_scatter | solution.py:39
  126.4 4.6 %fusion.38 = (bf16[256,1024]{1,0:T(8,128)(2,1)}, bf16[256,1024]{1,0:T(8,128)(2,1)}) fusion(bf16[256,1024]{1,0:T(8,128)(2,1)} %reduce-scatter.3.cloned.1.call-done, bf16[256,1024]{1,0:T(8,128)(2,1)} %reduce-scatter.5.cloned.1.call-done), kind=kLoop, calls=%fused_computation.52 | loop fusion | flops 20185088 | bytes 2097152 | tf_op jit(solution)/shard_map/convert_element_type | solution.py:61
  131.0 0.0 all-gather.6.cloned.1.call-update
  131.0 0.0 all-gather.8.cloned.1.call-start
  131.1 0.7 all-gather.8.cloned.1.call-update
  131.8 33.5 %all-gather.6.cloned.1.call-done = bf16[2048,1024]{1,0:T(8,128)(2,1)} async-done(((bf16[256,1024]{1,0:T(8,128)(2,1)}), bf16[2048,1024]{1,0:T(8,128)(2,1)}) %all-gather.6.cloned.1.call-update) | async-done | bytes 4194320 | tf_op jit(solution)/shard_map/all_gather | solution.py:25
  165.3 5.8 %convolution_convert_fusion.3 = bf16[2048,512]{1,0:T(8,128)(2,1)} fusion(bf16[2048,1024]{1,0:T(8,128)(2,1)} %all-gather.6.cloned.1.call-done, bf16[1024,512]{1,0:T(8,128)(2,1)S(1)} %copy-done), kind=kOutput, calls=%fused_computation.5 | convolution fusion | flops 2148532224 | bytes 7340032 | tf_op jit(solution)/shard_map/dot_general | solution.py:49
  171.1 6.7 %all-to-all-start = ((bf16[16,128,512]{2,1,0:T(8,128)(2,1)}), bf16[16,128,512]{2,1,0:T(8,128)(2,1)S(1)}, u32[]{:S(2)}, u32[]{:S(2)}) async-start(bf16[16,128,512]{2,1,0:T(8,128)(2,1)} %bitcast.24), calls=%async_computation.1 | async-start | bytes 4194304 | tf_op jit(solution)/shard_map/all_to_all | solution.py:51
  177.9 21.7 %all-gather.8.cloned.1.call-done = bf16[2048,1024]{1,0:T(8,128)(2,1)} async-done(((bf16[256,1024]{1,0:T(8,128)(2,1)}), bf16[2048,1024]{1,0:T(8,128)(2,1)}) %all-gather.8.cloned.1.call-update) | async-done | bytes 4194320 | tf_op jit(solution)/shard_map/all_gather | solution.py:25
  199.5 6.2 %convolution_convert_fusion.2 = bf16[2048,512]{1,0:T(8,128)(2,1)} fusion(bf16[2048,1024]{1,0:T(8,128)(2,1)} %all-gather.8.cloned.1.call-done, bf16[512,1024]{1,0:T(8,128)(2,1)} %param.5), kind=kOutput, calls=%fused_computation.4 | convolution fusion | flops 2148532224 | bytes 7340032 | tf_op jit(solution)/shard_map/dot_general | solution.py:29
  205.7 1.4 all-to-all-done
  207.1 5.4 %all-to-all-start.3 = ((bf16[16,128,512]{2,1,0:T(8,128)(2,1)}), bf16[16,128,512]{2,1,0:T(8,128)(2,1)}, u32[]{:S(2)}, u32[]{:S(2)}) async-start(bf16[16,128,512]{2,1,0:T(8,128)(2,1)} %bitcast.23), calls=%async_computation.5 | async-start | bytes 4194304 | tf_op jit(solution)/shard_map/all_to_all | solution.py:51
  212.5 6.6 %convolution_bitcast_fusion = f32[512,1024]{0,1:T(8,128)} fusion(bf16[2048,1024]{1,0:T(8,128)(2,1)} %all-gather.8.cloned.1.call-done, bf16[2048,512]{1,0:T(8,128)(2,1)} %all-gather.4.cloned.1.call-done), kind=kOutput, calls=%fused_computation.12 | convolution fusion | flops 2147483648 | bytes 8388608 | tf_op jit(solution)/shard_map/dot_general | solution.py:68
  219.0 2.9 %copy.12 = f32[512,1024]{1,0:T(8,128)} copy(f32[512,1024]{0,1:T(8,128)} %convolution_bitcast_fusion) | data formatting | bytes 4194304
  221.9 6.5 %fusion.39 = f32[1024,512]{1,0:T(8,128)} fusion(bf16[2048,1024]{1,0:T(8,128)(2,1)} %all-gather.6.cloned.1.call-done, bf16[2048,512]{1,0:T(8,128)(2,1)} %bitcast.22), kind=kOutput, calls=%fused_computation.55 | convolution fusion | flops 2147483648 | bytes 8388608 | tf_op jit(solution)/shard_map/dot_general | solution.py:65
  228.5 0.0 copy-start.3
  228.5 0.3 convert_reduce_fusion.1
  228.8 0.6 copy-done.3
  229.4 0.0 copy-start.2
  229.4 0.7 add_convert_fusion.1
  230.0 8.0 %all-to-all-done.3 = bf16[16,128,512]{2,1,0:T(8,128)(2,1)} async-done(((bf16[16,128,512]{2,1,0:T(8,128)(2,1)}), bf16[16,128,512]{2,1,0:T(8,128)(2,1)}, u32[]{:S(2)}, u32[]{:S(2)}) %all-to-all-start.3) | async-done | bytes 2097184 | tf_op jit(solution)/shard_map/all_to_all | solution.py:51
  238.1 8.6 %all-to-all-start.1 = ((bf16[8,16,512]{2,1,0:T(8,128)(2,1)}), bf16[8,16,512]{2,1,0:T(8,128)(2,1)S(1)}, u32[]{:S(2)}, u32[]{:S(2)}) async-start(bf16[8,16,512]{2,1,0:T(8,128)(2,1)} %bitcast.1), calls=%async_computation.2 | async-start | bytes 262144 | tf_op jit(solution)/shard_map/all_to_all | solution.py:64
  246.7 1.9 convert_reduce_fusion
  248.6 0.0 copy-done.2
  248.6 0.7 add_convert_fusion
  249.3 2.7 %all-to-all-done.1 = bf16[8,16,512]{2,1,0:T(8,128)(2,1)S(1)} async-done(((bf16[8,16,512]{2,1,0:T(8,128)(2,1)}), bf16[8,16,512]{2,1,0:T(8,128)(2,1)S(1)}, u32[]{:S(2)}, u32[]{:S(2)}) %all-to-all-start.1) | async-done | bytes 131104 | tf_op jit(solution)/shard_map/all_to_all | solution.py:64
  252.0 0.7 copy.13
Async XLA Ops:
  8.0 40.9 %copy-start = (bf16[1024,512]{1,0:T(8,128)(2,1)S(1)}, bf16[1024,512]{1,0:T(8,128)(2,1)}, u32[]{:S(2)}) copy-start(bf16[1024,512]{1,0:T(8,128)(2,1)} %param.6) | copy-start | bytes 3145732
  8.0 57.8 %all-gather.4.cloned.1.call-start = ((), (), s32[]{:S(2)}) async-start(), calls=%async_computation.6 | async-start | bytes 2228224 | tf_op jit(solution)/shard_map/all_gather | solution.py:14
  8.7 78.9 %reduce-scatter.5.cloned.1.call-start = ((), (), s32[]{:S(2)}) async-start(), calls=%async_computation.9 | async-start | bytes 4718592 | tf_op jit(solution)/shard_map/reduce_scatter | solution.py:39
  47.5 1.4 copy-start.1
  53.2 12.6 %copy-start.4 = (bf16[512,1024]{1,0:T(8,128)(2,1)S(1)}, bf16[512,1024]{1,0:T(8,128)(2,1)}, u32[]{:S(2)}) copy-start(bf16[512,1024]{1,0:T(8,128)(2,1)} %param.5) | copy-start | bytes 3145732
  53.3 73.2 %reduce-scatter.3.cloned.1.call-start = ((), (), s32[]{:S(2)}) async-start(), calls=%async_computation.7 | async-start | bytes 4718592 | tf_op jit(solution)/shard_map/reduce_scatter | solution.py:39
  71.8 93.5 %all-gather.6.cloned.1.call-start = ((), (), s32[]{:S(2)}) async-start(), calls=%async_computation.8 | async-start | bytes 4718592 | tf_op jit(solution)/shard_map/all_gather | solution.py:25
  131.0 68.5 %all-gather.8.cloned.1.call-start = ((), (), s32[]{:S(2)}) async-start(), calls=%async_computation.10 | async-start | bytes 4718592 | tf_op jit(solution)/shard_map/all_gather | solution.py:25
  171.1 35.9 %all-to-all-start = ((bf16[16,128,512]{2,1,0:T(8,128)(2,1)}), bf16[16,128,512]{2,1,0:T(8,128)(2,1)S(1)}, u32[]{:S(2)}, u32[]{:S(2)}) async-start(bf16[16,128,512]{2,1,0:T(8,128)(2,1)} %bitcast.24), calls=%async_computation.1 | async-start | bytes 4194304 | tf_op jit(solution)/shard_map/all_to_all | solution.py:51
  207.1 31.0 %all-to-all-start.3 = ((bf16[16,128,512]{2,1,0:T(8,128)(2,1)}), bf16[16,128,512]{2,1,0:T(8,128)(2,1)}, u32[]{:S(2)}, u32[]{:S(2)}) async-start(bf16[16,128,512]{2,1,0:T(8,128)(2,1)} %bitcast.23), calls=%async_computation.5 | async-start | bytes 4194304 | tf_op jit(solution)/shard_map/all_to_all | solution.py:51
  228.5 0.9 copy-start.3
  229.4 19.2 %copy-start.2 = (bf16[128,512]{1,0:T(8,128)(2,1)S(1)}, bf16[128,512]{1,0:T(8,128)(2,1)}, u32[]{:S(2)}) copy-start(bf16[128,512]{1,0:T(8,128)(2,1)} %param.7) | copy-start | bytes 393220
  238.1 13.9 %all-to-all-start.1 = ((bf16[8,16,512]{2,1,0:T(8,128)(2,1)}), bf16[8,16,512]{2,1,0:T(8,128)(2,1)S(1)}, u32[]{:S(2)}, u32[]{:S(2)}) async-start(bf16[8,16,512]{2,1,0:T(8,128)(2,1)} %bitcast.1), calls=%async_computation.2 | async-start | bytes 262144 | tf_op jit(solution)/shard_map/all_to_all | solution.py:64
Sparse Core Ops, SparseCore 0:
  11.0 54.8 all-gather.3
Sparse Core Ops, SparseCore 1:
  53.4 34.3 reduce-scatter.4
  89.9 36.4 reduce-scatter.2
  131.1 34.1 all-gather.5
  167.6 31.9 all-gather.7
where the time goes:
time: 261 us; the launch traced here: 260 us
  waiting for transfers between devices  136 us (52%)
  blocking collectives  37.6 us (14%)
  matrix products  35.4 us (14%)
  starting transfers between devices  20.9 us (8%)
  between operations  15.7 us (6%)
  other arithmetic  8.13 us (3%)
  local copies, waits for them, and re-layouts  6.64 us (3%)
    all_gather x2, waiting for transfers between devices, hidden_panel(): return lax.all_gather(local_rows, 'col', axis=0, tiled=True)  55.2 us
    reduce_scatter x2, waiting for transfers between devices, width_split(): lax.psum_scatter(term.astype(jnp.bfloat16), 'col', scatter_dimension=0, t...  54.6 us
    all_to_all x1, blocking collectives, token_panel_a2a(): lax.all_to_all(copies, 'row', split_axis=0, concat_axis=0, tiled=True)  37.6 us
    all_gather x1, waiting for transfers between devices, token_panel(): return lax.all_gather(local_rows, 'row', axis=0, tiled=True)  12.5 us
    all_to_all x2, starting transfers between devices, unit_sum(): lax.all_to_all(pieces, 'row', split_axis=0, concat_axis=0, tiled=True)  12.1 us
    dot_general x2, matrix products, contract_last(): lax.dot_general(left, right, (((1,), (1,)), ((), ())), preferred_element_...  10.5 us
    all_to_all x2, waiting for transfers between devices, unit_sum(): lax.all_to_all(pieces, 'row', split_axis=0, concat_axis=0, tiled=True)  9.4 us
    all_to_all x1, starting transfers between devices, local(): lax.all_to_all(block_rows, 'col', split_axis=0, concat_axis=1, tiled=True)  8.57 us
  transfers between devices with their start and end apart: 8, of which 8 were waited for; matrix products, arithmetic and copies ran while one was open for 17% of the time, Pallas kernels for 0%

commit v1 on v0

--- a/solution.py
+++ b/solution.py
@@ -2,6 +2,22 @@
 import jax.numpy as jnp
 from jax import lax
 from jax.sharding import PartitionSpec as P
+
+
+def pairwise_exchange(x, axis, split, join):
+    ways, here = (lax.axis_size(axis), lax.axis_index(axis))
+    width = x.shape[split] // ways
+    dims = list(x.shape)
+    dims[split] = width
+    height = dims[join]
+    dims[join] = height * ways
+    full = jnp.zeros(dims, x.dtype)
+    for mask in range(ways):
+        part = lax.dynamic_slice_in_dim(x, (here ^ mask) * width, width, axis=split)
+        if mask:
+            part = lax.ppermute(part, axis, [(d, d ^ mask) for d in range(ways)])
+        full = lax.dynamic_update_slice_in_dim(full, part, (here ^ mask) * height, axis=join)
+    return full
 
 
 def gelu_grad(value):
@@ -61,7 +77,7 @@
     dpre_all = hidden_panel((dact_part * gelu_grad(pre_part)).astype(jnp.bfloat16))
     mixed = unit_sum(act_all, w_out, False)
     block_rows = (tokens.astype(jnp.float32) + mixed).astype(jnp.bfloat16)
-    block_out = lax.all_to_all(block_rows, "col", split_axis=0, concat_axis=1, tiled=True)
+    block_out = pairwise_exchange(block_rows, "col", 0, 1)
     grad_out = lax.dot_general(
         act_all, upstream_all, (((0,), (0,)), ((), ())), preferred_element_type=jnp.float32
     )

time: 261 us -> 266 us (1.019)
  starting transfers between devices: 20.9 us -> 26.7 us
    ppermute x0 -> x7, starting transfers between devices: none -> 14.4 us  [pairwise_exchange(): part = lax.ppermute(part, axis, [(d, d ^ mask) for d in range(ways)])]
    all_to_all x1 -> x0, starting transfers between devices: 8.57 us -> none  [local(): lax.all_to_all(block_rows, 'col', split_axis=0, concat_axis=1, tiled=True)]
    ppermute x0 -> x7, waiting for transfers between devices: none -> 3.49 us  [pairwise_exchange(): part = lax.ppermute(part, axis, [(d, d ^ mask) for d in range(ways)])]
    all_to_all x1 -> x0, waiting for transfers between devices: 2.68 us -> none  [local(): lax.all_to_all(block_rows, 'col', split_axis=0, concat_axis=1, tiled=True)]
    unnamed x11 -> x17, local copies, waits for them, and re-layouts: 4.88 us -> 6.87 us
  transfers between devices with their start and end apart: 8 -> 14, of which waited for: 8 -> 9; matrix products, arithmetic and copies ran while one was open for 17% -> 15% of each run, Pallas kernels for 0% -> 0%
where the time goes in v1:
time: 266 us; the launch traced here: 265 us
  waiting for transfers between devices  136 us (51%)
  blocking collectives  37.6 us (14%)
  matrix products  35.6 us (13%)
  starting transfers between devices  26.7 us (10%)
  between operations  15.9 us (6%)
  local copies, waits for them, and re-layouts  8.06 us (3%)
  other arithmetic  5.86 us (2%)
    all_gather x2, waiting for transfers between devices, hidden_panel(): return lax.all_gather(local_rows, 'col', axis=0, tiled=True)  55.2 us
    reduce_scatter x2, waiting for transfers between devices, width_split(): lax.psum_scatter(term.astype(jnp.bfloat16), 'col', scatter_dimension=0, t...  54.6 us
    all_to_all x1, blocking collectives, token_panel_a2a(): lax.all_to_all(copies, 'row', split_axis=0, concat_axis=0, tiled=True)  37.6 us
    ppermute x7, starting transfers between devices, pairwise_exchange(): part = lax.ppermute(part, axis, [(d, d ^ mask) for d in range(ways)])  14.4 us
    all_gather x1, waiting for transfers between devices, token_panel(): return lax.all_gather(local_rows, 'row', axis=0, tiled=True)  12.5 us
    all_to_all x2, starting transfers between devices, unit_sum(): lax.all_to_all(pieces, 'row', split_axis=0, concat_axis=0, tiled=True)  12.1 us
    dot_general x2, matrix products, contract_last(): lax.dot_general(left, right, (((1,), (1,)), ((), ())), preferred_element_...  10.5 us
    all_to_all x2, waiting for transfers between devices, unit_sum(): lax.all_to_all(pieces, 'row', split_axis=0, concat_axis=0, tiled=True)  8.26 us
  transfers between devices with their start and end apart: 14, of which 9 were waited for; matrix products, arithmetic and copies ran while one was open for 15% of the time, Pallas kernels for 0%

profile of v1, /device:TPU:1, one launch (start us, length us, event | category | flops | bytes accessed | tf_op | source)
XLA Modules:
  0.0 265.2 jit_solution(11316369498597218609)
XLA Ops:
  8.0 0.0 copy-start
  8.0 0.0 all-gather.4.cloned.1.call-start
  8.1 0.7 all-gather.4.cloned.1.call-update
  8.7 0.0 reduce-scatter.5.cloned.1.call-start
  8.8 1.1 broadcast_in_dim.10
  9.9 37.6 %all_to_all.19 = bf16[16,128,512]{2,1,0:T(8,128)(2,1)S(1)} all-to-all(bf16[16,128,512]{2,1,0:T(8,128)(2,1)S(1)} %broadcast_in_dim.10), channel_id=1, replica_groups=mesh['row'=16,'col'=8] {'row'}, dimensions={0} | all-to-all | bytes 4194304 | tf_op jit(solution)/shard_map/all_to_all | solution.py:37
  47.5 0.0 copy-start.3
  47.5 1.4 copy-done.3
  48.9 0.0 copy-done
  48.9 4.3 %convolution_convert_fusion = bf16[2048,1024]{1,0:T(8,128)(2,1)} fusion(bf16[2048,512]{1,0:T(8,128)(2,1)S(1)} %bitcast.17, bf16[1024,512]{1,0:T(8,128)(2,1)S(1)} %copy-done), kind=kOutput, calls=%fused_computation.2 | convolution fusion | flops 2149580800 | bytes 7340032 | tf_op jit(solution)/shard_map/dot_general | solution.py:45
  53.3 0.0 copy-start.7
  53.3 0.0 reduce-scatter.5.cloned.1.call-update
  53.3 0.0 reduce-scatter.3.cloned.1.call-start
  53.3 12.5 %all-gather.4.cloned.1.call-done = bf16[2048,512]{1,0:T(8,128)(2,1)} async-done(((bf16[128,512]{1,0:T(8,128)(2,1)}), bf16[2048,512]{1,0:T(8,128)(2,1)}) %all-gather.4.cloned.1.call-update) | async-done | bytes 2097168 | tf_op jit(solution)/shard_map/all_gather | solution.py:30
  65.8 0.0 copy-done.7
  65.8 6.0 %convolution_convert_fusion.1 = bf16[2048,1024]{1,0:T(8,128)(2,1)} fusion(bf16[2048,512]{1,0:T(8,128)(2,1)} %all-gather.4.cloned.1.call-done, bf16[512,1024]{1,0:T(8,128)(2,1)S(1)} %copy-done.7), kind=kOutput, calls=%fused_computation.3 | convolution fusion | flops 2149580800 | bytes 7340032 | tf_op jit(solution)/shard_map/dot_general | solution.py:54
  71.8 0.0 reduce-scatter.3.cloned.1.call-update
  71.8 0.0 all-gather.6.cloned.1.call-start
  71.9 15.8 %reduce-scatter.5.cloned.1.call-done = bf16[256,1024]{1,0:T(8,128)(2,1)} async-done(((bf16[2048,1024]{1,0:T(8,128)(2,1)}), bf16[256,1024]{1,0:T(8,128)(2,1)}) %reduce-scatter.5.cloned.1.call-update) | async-done | bytes 524304 | tf_op jit(solution)/shard_map/reduce_scatter | solution.py:55
  87.7 38.9 %reduce-scatter.3.cloned.1.call-done = bf16[256,1024]{1,0:T(8,128)(2,1)} async-done(((bf16[2048,1024]{1,0:T(8,128)(2,1)}), bf16[256,1024]{1,0:T(8,128)(2,1)}) %reduce-scatter.3.cloned.1.call-update) | async-done | bytes 524304 | tf_op jit(solution)/shard_map/reduce_scatter | solution.py:55
  126.5 4.6 %fusion.38 = (bf16[256,1024]{1,0:T(8,128)(2,1)}, bf16[256,1024]{1,0:T(8,128)(2,1)}) fusion(bf16[256,1024]{1,0:T(8,128)(2,1)} %reduce-scatter.3.cloned.1.call-done, bf16[256,1024]{1,0:T(8,128)(2,1)} %reduce-scatter.5.cloned.1.call-done), kind=kLoop, calls=%fused_computation.52 | loop fusion | flops 20185088 | bytes 2097152 | tf_op jit(solution)/shard_map/convert_element_type | solution.py:77
  131.1 0.0 all-gather.6.cloned.1.call-update
  131.1 0.0 all-gather.8.cloned.1.call-start
  131.2 0.7 all-gather.8.cloned.1.call-update
  131.9 33.5 %all-gather.6.cloned.1.call-done = bf16[2048,1024]{1,0:T(8,128)(2,1)} async-done(((bf16[256,1024]{1,0:T(8,128)(2,1)}), bf16[2048,1024]{1,0:T(8,128)(2,1)}) %all-gather.6.cloned.1.call-update) | async-done | bytes 4194320 | tf_op jit(solution)/shard_map/all_gather | solution.py:41
  165.4 5.9 %convolution_convert_fusion.3 = bf16[2048,512]{1,0:T(8,128)(2,1)} fusion(bf16[2048,1024]{1,0:T(8,128)(2,1)} %all-gather.6.cloned.1.call-done, bf16[1024,512]{1,0:T(8,128)(2,1)S(1)} %copy-done), kind=kOutput, calls=%fused_computation.5 | convolution fusion | flops 2148532224 | bytes 7340032 | tf_op jit(solution)/shard_map/dot_general | solution.py:65
  171.3 6.7 %all-to-all-start = ((bf16[16,128,512]{2,1,0:T(8,128)(2,1)}), bf16[16,128,512]{2,1,0:T(8,128)(2,1)S(1)}, u32[]{:S(2)}, u32[]{:S(2)}) async-start(bf16[16,128,512]{2,1,0:T(8,128)(2,1)} %bitcast.20), calls=%async_computation.1 | async-start | bytes 4194304 | tf_op jit(solution)/shard_map/all_to_all | solution.py:67
  178.0 21.7 %all-gather.8.cloned.1.call-done = bf16[2048,1024]{1,0:T(8,128)(2,1)} async-done(((bf16[256,1024]{1,0:T(8,128)(2,1)}), bf16[2048,1024]{1,0:T(8,128)(2,1)}) %all-gather.8.cloned.1.call-update) | async-done | bytes 4194320 | tf_op jit(solution)/shard_map/all_gather | solution.py:41
  199.6 6.2 %convolution_convert_fusion.2 = bf16[2048,512]{1,0:T(8,128)(2,1)} fusion(bf16[2048,1024]{1,0:T(8,128)(2,1)} %all-gather.8.cloned.1.call-done, bf16[512,1024]{1,0:T(8,128)(2,1)} %param.5), kind=kOutput, calls=%fused_computation.4 | convolution fusion | flops 2148532224 | bytes 7340032 | tf_op jit(solution)/shard_map/dot_general | solution.py:45
  205.8 1.3 all-to-all-done
  207.1 0.0 copy-start.1
  207.1 1.3 copy-done.1
  208.5 5.4 %all-to-all-start.2 = ((bf16[16,128,512]{2,1,0:T(8,128)(2,1)}), bf16[16,128,512]{2,1,0:T(8,128)(2,1)S(1)}, u32[]{:S(2)}, u32[]{:S(2)}) async-start(bf16[16,128,512]{2,1,0:T(8,128)(2,1)} %bitcast.19), calls=%async_computation.4 | async-start | bytes 4194304 | tf_op jit(solution)/shard_map/all_to_all | solution.py:67
  213.9 6.5 %convolution_bitcast_fusion = f32[512,1024]{0,1:T(8,128)} fusion(bf16[2048,1024]{1,0:T(8,128)(2,1)} %all-gather.8.cloned.1.call-done, bf16[2048,512]{1,0:T(8,128)(2,1)} %all-gather.4.cloned.1.call-done), kind=kOutput, calls=%fused_computation.12 | convolution fusion | flops 2147483648 | bytes 8388608 | tf_op jit(solution)/shard_map/dot_general | solution.py:84
  220.5 2.9 %copy.8 = f32[512,1024]{1,0:T(8,128)} copy(f32[512,1024]{0,1:T(8,128)} %convolution_bitcast_fusion) | data formatting | bytes 4194304
  223.4 0.0 copy-start.2
  223.4 6.7 %fusion.39 = f32[1024,512]{1,0:T(8,128)} fusion(bf16[2048,1024]{1,0:T(8,128)(2,1)} %all-gather.6.cloned.1.call-done, bf16[2048,512]{1,0:T(8,128)(2,1)} %bitcast.18), kind=kOutput, calls=%fused_computation.70 | convolution fusion | flops 2147483648 | bytes 8388608 | tf_op jit(solution)/shard_map/dot_general | solution.py:81
  230.0 0.0 copy-done.2
  230.0 0.0 copy-start.5
  230.0 0.3 convert_reduce_fusion.1
  230.3 0.6 copy-done.5
  230.9 0.0 copy-start.4
  231.0 1.5 collective-permute-start
  232.5 6.9 %all-to-all-done.2 = bf16[16,128,512]{2,1,0:T(8,128)(2,1)S(1)} async-done(((bf16[16,128,512]{2,1,0:T(8,128)(2,1)}), bf16[16,128,512]{2,1,0:T(8,128)(2,1)S(1)}, u32[]{:S(2)}, u32[]{:S(2)}) %all-to-all-start.2) | async-done | bytes 2097184 | tf_op jit(solution)/shard_map/all_to_all | solution.py:67
  239.4 0.3 convert_reduce_fusion
  239.7 0.0 copy-done.4
  239.7 0.7 add_convert_fusion
  240.4 5.7 %collective-permute-start.6 = (bf16[16,512]{1,0:T(8,128)(2,1)S(1)}, bf16[16,512]{1,0:T(8,128)(2,1)S(1)}, u32[]{:S(2)}, u32[]{:S(2)}) collective-permute-start(bf16[16,512]{1,0:T(8,128)(2,1)S(1)} %get-tuple-element.10), channel_id=1, source_target_pairs={{0,7},{1,6},{2,5},{3,4},{4,3},{5,2},{6,1},{7,0},{8,15},{9,14},{10,... | collective-permute-start | bytes 49160 | tf_op jit(solution)/shard_map/ppermute | solution.py:18
  246.1 2.1 collective-permute-start.5
  248.3 0.0 collective-permute-start.4
  248.3 1.1 collective-permute-start.3
  249.4 0.0 collective-permute-done
  249.4 0.6 collective-permute-start.1
  250.0 2.1 collective-permute-done.1
  252.0 3.4 %collective-permute-start.2 = (bf16[16,512]{1,0:T(8,128)(2,1)S(1)}, bf16[16,512]{1,0:T(8,128)(2,1)S(1)}, u32[]{:S(2)}, u32[]{:S(2)}) collective-permute-start(bf16[16,512]{1,0:T(8,128)(2,1)S(1)} %get-tuple-element.14), channel_id=1, source_target_pairs={{0,3},{1,2},{2,1},{3,0},{4,7},{5,6},{6,5},{7,4},{8,11},{9,10},{10,... | collective-permute-start | bytes 49160 | tf_op jit(solution)/shard_map/ppermute | solution.py:18
  255.5 1.4 collective-permute-done.2
  256.9 0.0 collective-permute-done.3
  256.9 0.0 collective-permute-done.4
  256.9 0.0 collective-permute-done.5
  256.9 0.0 collective-permute-done.6
  257.0 0.0 copy-start.6
  257.0 0.6 copy-done.6
  (10 shorter events, 0.1 us)
Async XLA Ops:
  8.0 40.9 %copy-start = (bf16[1024,512]{1,0:T(8,128)(2,1)S(1)}, bf16[1024,512]{1,0:T(8,128)(2,1)}, u32[]{:S(2)}) copy-start(bf16[1024,512]{1,0:T(8,128)(2,1)} %param.6) | copy-start | bytes 3145732
  8.0 57.8 %all-gather.4.cloned.1.call-start = ((), (), s32[]{:S(2)}) async-start(), calls=%async_computation.5 | async-start | bytes 2228224 | tf_op jit(solution)/shard_map/all_gather | solution.py:30
  8.7 78.9 %reduce-scatter.5.cloned.1.call-start = ((), (), s32[]{:S(2)}) async-start(), calls=%async_computation.8 | async-start | bytes 4718592 | tf_op jit(solution)/shard_map/reduce_scatter | solution.py:55
  47.5 1.4 copy-start.3
  53.3 12.6 %copy-start.7 = (bf16[512,1024]{1,0:T(8,128)(2,1)S(1)}, bf16[512,1024]{1,0:T(8,128)(2,1)}, u32[]{:S(2)}) copy-start(bf16[512,1024]{1,0:T(8,128)(2,1)} %param.5) | copy-start | bytes 3145732
  53.3 73.2 %reduce-scatter.3.cloned.1.call-start = ((), (), s32[]{:S(2)}) async-start(), calls=%async_computation.6 | async-start | bytes 4718592 | tf_op jit(solution)/shard_map/reduce_scatter | solution.py:55
  71.8 93.6 %all-gather.6.cloned.1.call-start = ((), (), s32[]{:S(2)}) async-start(), calls=%async_computation.7 | async-start | bytes 4718592 | tf_op jit(solution)/shard_map/all_gather | solution.py:41
  131.1 68.5 %all-gather.8.cloned.1.call-start = ((), (), s32[]{:S(2)}) async-start(), calls=%async_computation.9 | async-start | bytes 4718592 | tf_op jit(solution)/shard_map/all_gather | solution.py:41
  171.3 35.9 %all-to-all-start = ((bf16[16,128,512]{2,1,0:T(8,128)(2,1)}), bf16[16,128,512]{2,1,0:T(8,128)(2,1)S(1)}, u32[]{:S(2)}, u32[]{:S(2)}) async-start(bf16[16,128,512]{2,1,0:T(8,128)(2,1)} %bitcast.20), calls=%async_computation.1 | async-start | bytes 4194304 | tf_op jit(solution)/shard_map/all_to_all | solution.py:67
  207.1 1.3 copy-start.1
  208.5 31.0 %all-to-all-start.2 = ((bf16[16,128,512]{2,1,0:T(8,128)(2,1)}), bf16[16,128,512]{2,1,0:T(8,128)(2,1)S(1)}, u32[]{:S(2)}, u32[]{:S(2)}) async-start(bf16[16,128,512]{2,1,0:T(8,128)(2,1)} %bitcast.19), calls=%async_computation.4 | async-start | bytes 4194304 | tf_op jit(solution)/shard_map/all_to_all | solution.py:67
  223.4 6.7 %copy-start.2 = (bf16[16,128,512]{2,1,0:T(8,128)(2,1)S(1)}, bf16[16,128,512]{2,1,0:T(8,128)(2,1)}, u32[]{:S(2)}) copy-start(bf16[16,128,512]{2,1,0:T(8,128)(2,1)} %copy-done.1) | copy-start | bytes 6291460
  230.0 0.9 copy-start.5
  230.9 8.8 %copy-start.4 = (bf16[128,512]{1,0:T(8,128)(2,1)S(1)}, bf16[128,512]{1,0:T(8,128)(2,1)}, u32[]{:S(2)}) copy-start(bf16[128,512]{1,0:T(8,128)(2,1)} %param.7) | copy-start | bytes 393220
  231.0 18.4 %collective-permute-start = (bf16[16,512]{1,0:T(8,128)(2,1)S(1)}, bf16[16,512]{1,0:T(8,128)(2,1)S(1)}, u32[]{:S(2)}, u32[]{:S(2)}) collective-permute-start(bf16[16,512]{1,0:T(8,128)(2,1)S(1)} %get-tuple-element.16), channel_id=1, source_target_pairs={{0,1},{1,0},{2,3},{3,2},{4,5},{5,4},{6,7},{7,6},{8,9},{9,8},{10,11... | collective-permute-start | bytes 49160 | tf_op jit(solution)/shard_map/ppermute | solution.py:18
  240.4 16.5 %collective-permute-start.6 = (bf16[16,512]{1,0:T(8,128)(2,1)S(1)}, bf16[16,512]{1,0:T(8,128)(2,1)S(1)}, u32[]{:S(2)}, u32[]{:S(2)}) collective-permute-start(bf16[16,512]{1,0:T(8,128)(2,1)S(1)} %get-tuple-element.10), channel_id=1, source_target_pairs={{0,7},{1,6},{2,5},{3,4},{4,3},{5,2},{6,1},{7,0},{8,15},{9,14},{10,... | collective-permute-start | bytes 49160 | tf_op jit(solution)/shard_map/ppermute | solution.py:18
  246.1 10.8 %collective-permute-start.5 = (bf16[16,512]{1,0:T(8,128)(2,1)S(1)}, bf16[16,512]{1,0:T(8,128)(2,1)S(1)}, u32[]{:S(2)}, u32[]{:S(2)}) collective-permute-start(bf16[16,512]{1,0:T(8,128)(2,1)S(1)} %get-tuple-element.11), channel_id=1, source_target_pairs={{0,6},{1,7},{2,4},{3,5},{4,2},{5,3},{6,0},{7,1},{8,14},{9,15},{10,... | collective-permute-start | bytes 49160 | tf_op jit(solution)/shard_map/ppermute | solution.py:18
  248.3 8.6 %collective-permute-start.4 = (bf16[16,512]{1,0:T(8,128)(2,1)S(1)}, bf16[16,512]{1,0:T(8,128)(2,1)S(1)}, u32[]{:S(2)}, u32[]{:S(2)}) collective-permute-start(bf16[16,512]{1,0:T(8,128)(2,1)S(1)} %get-tuple-element.12), channel_id=1, source_target_pairs={{0,5},{1,4},{2,7},{3,6},{4,1},{5,0},{6,3},{7,2},{8,13},{9,12},{10,... | collective-permute-start | bytes 49160 | tf_op jit(solution)/shard_map/ppermute | solution.py:18
  248.3 8.6 %collective-permute-start.3 = (bf16[16,512]{1,0:T(8,128)(2,1)S(1)}, bf16[16,512]{1,0:T(8,128)(2,1)S(1)}, u32[]{:S(2)}, u32[]{:S(2)}) collective-permute-start(bf16[16,512]{1,0:T(8,128)(2,1)S(1)} %get-tuple-element.13), channel_id=1, source_target_pairs={{0,4},{1,5},{2,6},{3,7},{4,0},{5,1},{6,2},{7,3},{8,12},{9,13},{10,... | collective-permute-start | bytes 49160 | tf_op jit(solution)/shard_map/ppermute | solution.py:18
  249.4 2.6 collective-permute-start.1
  252.0 4.8 %collective-permute-start.2 = (bf16[16,512]{1,0:T(8,128)(2,1)S(1)}, bf16[16,512]{1,0:T(8,128)(2,1)S(1)}, u32[]{:S(2)}, u32[]{:S(2)}) collective-permute-start(bf16[16,512]{1,0:T(8,128)(2,1)S(1)} %get-tuple-element.14), channel_id=1, source_target_pairs={{0,3},{1,2},{2,1},{3,0},{4,7},{5,6},{6,5},{7,4},{8,11},{9,10},{10,... | collective-permute-start | bytes 49160 | tf_op jit(solution)/shard_map/ppermute | solution.py:18
  257.0 0.7 copy-start.6
Sparse Core Ops, SparseCore 0:
  11.0 54.8 all-gather.3
Sparse Core Ops, SparseCore 1:
  53.4 34.3 reduce-scatter.4
  90.0 36.5 reduce-scatter.2
  131.2 34.1 all-gather.5
  167.7 31.9 all-gather.7
